TPU v7x, 512 devices: a whole 4x8x8 slice. The times are simulated.
512 devices in a mesh: gx: 32 (over y_hi, z), az: 4 (over y_lo, core), ta: 4 (over x).
Axes of the slice: x: 4, y: 8 (y_hi: 4, y_lo: 2; y = y_hi * 2 + y_lo), z: 8, core: 2. Of those that a mesh axis runs over, the one named last changes fastest.
Arguments:
- velocity: float32 [512, 32, 1024], P('gx', 'az', 'ta'), may hold values from -6 to 6
- pressure: float32 [512, 32, 1024], P('gx', 'az', 'ta'), may hold values from -6 to 6
- offsets: int32 [8], replicated, may hold values from 1 to 16, as said below
Outputs:
- correlation: float32 [512, 8, 1056], P(('gx', 'az', 'ta'))
Inputs may be any that keep to these rules, and one draw needn't show every extreme that they name: `offsets`: the 8 separations are distinct and the largest equals 16.
All inputs are finite; a program needn't handle non-finite values.
Results may differ from a plain program's by a relative error of at most 0.00007.
Values sent between devices are 32-bit elements; how exact they have to be, the bound alone decides.
A program may use at most 64 MiB of HBM per device.

v0:
```python
import math

import jax
import jax.numpy as jnp
from jax import lax
from jax.sharding import PartitionSpec as P

AZIM = 32
NBR = 8
MAXLAG = 16
LAGS = 33


def from_behind(value, axis, steps):
    count = lax.axis_size(axis)
    leading, last = (max(0, -steps), min(count, count - steps))
    return lax.ppermute(value, axis, [(source, source + steps) for source in range(leading, last)])


def padded_2(block, sides, width):
    for axis, dim in sides:
        count = lax.axis_size(axis)
        forward = [(i, i + 1) for i in range(count - 1)]
        backward = [(target, source) for source, target in forward]
        low = lax.ppermute(
            lax.slice_in_dim(block, block.shape[dim] - width, None, axis=dim), axis, forward
        )
        high = lax.ppermute(lax.slice_in_dim(block, 0, width, axis=dim), axis, backward)
        block = jnp.concatenate([low, block, high], axis=dim)
    return block


def correlate(vel_block, pres_block, pres_first, offsets):
    sta_dev = vel_block.shape[0]
    vel_count = vel_block.shape[1]
    pres_count = pres_block.shape[1]
    window = pres_block.shape[2]
    lags_total = 2 * MAXLAG + 1
    group = 8
    blocks = sta_dev // group
    vel_rows = jnp.arange(vel_count, dtype=jnp.int32)
    pres_rows = jnp.arange(pres_count, dtype=jnp.int32) + pres_first
    spread = (pres_rows[None, :] - vel_rows[:, None]) % AZIM
    pairing = (spread[:, :, None] == jnp.arange(AZIM, dtype=jnp.int32)[None, None, :]).astype(
        jnp.float32
    )
    padded_vel = jnp.pad(vel_block, ((0, 0), (0, 0), (2 * MAXLAG, 2 * MAXLAG)))

    def one_block(block_id):
        first = block_id * group
        series = lax.dynamic_slice_in_dim(padded_vel, first, group, 0)
        stacked = jnp.stack(
            [
                series[:, :, 2 * MAXLAG - shift_lag : 2 * MAXLAG - shift_lag + window]
                for shift_lag in range(lags_total)
            ],
            axis=2,
        )
        stations = first + jnp.arange(group, dtype=jnp.int32)
        indices = (stations[:, None] + offsets[None, :]).reshape(-1)
        partners = jnp.take(pres_block, indices, axis=0).reshape(
            group, offsets.shape[0], pres_count, window
        )
        product = jnp.einsum("spjt,skqt->spjkq", stacked, partners, precision=lax.Precision.HIGHEST)
        return jnp.einsum("spjkq,pqd->skjd", product, pairing, precision=lax.Precision.HIGHEST)

    results = lax.map(one_block, jnp.arange(blocks, dtype=jnp.int32))
    return results.reshape(sta_dev, offsets.shape[0], lags_total, AZIM)


def shards(velocity, pressure, offsets):
    sta_dev, az_dev, time_dev = velocity.shape
    factor = 1.0 / math.sqrt(time_dev * lax.axis_size("ta") * AZIM)
    own_first = lax.axis_index("az") * az_dev
    ahead_rows = from_behind(pressure, "gx", -1)
    extended = jnp.concatenate([pressure, ahead_rows], axis=0)
    padded = padded_2(extended, (("ta", 2),), MAXLAG)
    totals = correlate(
        lax.all_gather(velocity, "az", axis=1, tiled=True), padded, own_first, offsets
    )
    partial_value = (totals * factor).reshape(sta_dev, NBR, LAGS * AZIM)
    result = lax.psum_scatter(partial_value, ("az", "ta"), scatter_dimension=0, tiled=True)
    return result


def solution(mesh):
    return jax.shard_map(
        shards,
        mesh=mesh,
        in_specs=(P("gx", "az", "ta"), P("gx", "az", "ta"), P()),
        out_specs=P(("gx", "az", "ta"), None, None),
        check_vma=False,
    )
```

profile of v0, /device:TPU:1, one launch (start us, length us, event | category | flops | bytes accessed | tf_op | source)
XLA Modules:
  0.0 318.1 jit_solution(7849421964464386820)
XLA Ops:
  6.5 1.3 collective-permute-start
  8.8 5.1 %collective-permute-done = f32[16,8,256]{2,1,0:T(8,128)S(1)} collective-permute-done((f32[16,8,256]{2,1,0:T(8,128)}, f32[16,8,256]{2,1,0:T(8,128)S(1)}, u32[]{:S(2)}, u32[]{:S(2)}) %collective-permute-start) | collective-permute-done | bytes 131104 | tf_op jit(solution)/shard_map/ppermute | solution.py:17
  14.0 4.0 %collective-permute-start.1 = (f32[32,8,16]{2,1,0:T(8,128)S(1)}, f32[32,8,16]{2,1,0:T(8,128)S(1)}, u32[]{:S(2)}, u32[]{:S(2)}) collective-permute-start(f32[32,8,16]{2,1,0:T(8,128)S(1)} %get-tuple-element.74), channel_id=1, source_target_pairs={{0,1},{1,2},{2,3},{4,5},{5,6},{6,7},{8,9},{9,10},{10,11},{12,13},{... | collective-permute-start | bytes 49160 | tf_op jit(solution)/shard_map/ppermute | solution.py:25
  18.0 1.3 collective-permute-start.2
  19.3 10.5 %all_gather.3 = f32[16,32,256]{2,1,0:T(8,128)S(1)} all-gather(f32[16,8,256]{2,1,0:T(8,128)} %param.5), channel_id=1, replica_groups=mesh['gx'=32,'az'=4,'ta'=4] {'az'}, dimensions={1}, use_global_device_ids=true | all-gather | bytes 655360 | tf_op jit(solution)/shard_map/all_gather | solution.py:79
  30.3 200.8 %while.11 = (s32[]{:T(128)}, f32[2,8,8,33,32]{3,4,2,1,0:T(8,128)}, s32[2]{0:T(128)S(1)}, f32[16,32,320]{2,1,0:T(8,128)S(1)}, s32[8]{0:T(128)}, /*index=5*/f32[32...) while((s32[]{:T(128)}, f32[2,8,8,33,32]{3,4,2,1,0:T(8,128)}, ...), condition=%wide.region_1.2_spmd.clone, body=%wide.region_0.1_spmd.clone.sunk | while | flops 2076346112 | bytes 39592680 | solution.py:67
  32.5 1.0 fusion.104
  37.2 1.0 fusion.109
  42.8 1.0 fusion.115
  51.2 1.0 fusion.124
  57.8 1.0 fusion.131
  63.3 44.0 %fusion.137 = f32[8,32,33,8,8]{1,4,3,2,0:T(8,128)S(1)} fusion(f32[8,32,33,288]{3,1,2,0:T(8,128)} %fusion.135, f32[8,8,8,288]{3,2,1,0:T(8,128)S(1)} %bitcast.305, pred[8,8]{1,0:T(8,128)(4,1)S(1)} %compare_and_fusion.2), kind=kOutput, calls=%fused_computation.2.clone.1 | convolution fusion | flops 1868709888 | bytes 12484672 | tf_op jit(solution)/shard_map/while/body/eval_jaxpr/spjt,skqt->spjkq/dot_general | solution.py:64
  107.3 23.5 %fusion.138 = f32[2,8,8,33,32]{3,4,2,1,0:T(8,128)} fusion(f32[2,8,8,33,32]{3,4,2,1,0:T(8,128)} %get-tuple-element.163, s32[]{:T(128)} %get-tuple-element.162, f32[8,32,33,8,8]{1,4,3,2,0:T(8,128)S(1)} %fusion.137, s32[32,8]{0,1:T(8,128)S(1)} %get-tuple-element.211), kind=kOutput, calls=%fused_computation.7.clone.1 | convolution fusion | flops 207634432 | bytes 3212800 | tf_op jit(solution)/shard_map/while/body/eval_jaxpr/spjkq,pqd->skjd/dot_general | solution.py:65
  132.9 1.0 fusion.104
  137.6 1.0 fusion.109
  143.2 1.0 fusion.115
  151.6 1.0 fusion.124
  158.2 1.0 fusion.131
  163.7 44.0 %fusion.137 = f32[8,32,33,8,8]{1,4,3,2,0:T(8,128)S(1)} fusion(f32[8,32,33,288]{3,1,2,0:T(8,128)} %fusion.135, f32[8,8,8,288]{3,2,1,0:T(8,128)S(1)} %bitcast.305, pred[8,8]{1,0:T(8,128)(4,1)S(1)} %compare_and_fusion.2), kind=kOutput, calls=%fused_computation.2.clone.1 | convolution fusion | flops 1868709888 | bytes 12484672 | tf_op jit(solution)/shard_map/while/body/eval_jaxpr/spjt,skqt->spjkq/dot_general | solution.py:64
  207.7 23.4 %fusion.138 = f32[2,8,8,33,32]{3,4,2,1,0:T(8,128)} fusion(f32[2,8,8,33,32]{3,4,2,1,0:T(8,128)} %get-tuple-element.163, s32[]{:T(128)} %get-tuple-element.162, f32[8,32,33,8,8]{1,4,3,2,0:T(8,128)S(1)} %fusion.137, s32[32,8]{0,1:T(8,128)S(1)} %get-tuple-element.211), kind=kOutput, calls=%fused_computation.7.clone.1 | convolution fusion | flops 207634432 | bytes 3212800 | tf_op jit(solution)/shard_map/while/body/eval_jaxpr/spjkq,pqd->skjd/dot_general | solution.py:65
  231.1 3.2 %broadcast_multiply_fusion = f32[2,8,8,33,32]{3,4,2,1,0:T(8,128)} fusion(f32[2,8,8,33,32]{3,4,2,1,0:T(8,128)} %get-tuple-element.42), kind=kLoop, calls=%fused_computation.90 | loop fusion | flops 135168 | bytes 1081344 | tf_op jit(solution)/shard_map/mul | solution.py:81
  234.3 2.3 copy.39
  236.6 1.4 mul.22
  238.0 73.2 %reduce-scatter.5.cloned.1.call-done = f32[1,8,1056]{2,1,0:T(8,128)} async-done(((f32[16,8,1056]{2,1,0:T(8,128)}), f32[1,8,1056]{2,1,0:T(8,128)}) %reduce-scatter.5.cloned.1.call-update) | async-done | bytes 33808
  (89 shorter events, 56.5 us)
Async XLA Ops:
  6.5 304.7 %reduce-scatter.5.cloned.1.call-start = ((), (), s32[]{:S(2)}) async-start(), calls=%async_computation.1 | async-start | bytes 626688
  6.5 7.4 %collective-permute-start = (f32[16,8,256]{2,1,0:T(8,128)}, f32[16,8,256]{2,1,0:T(8,128)S(1)}, u32[]{:S(2)}, u32[]{:S(2)}) collective-permute-start(f32[16,8,256]{2,1,0:T(8,128)} %param.6), channel_id=1, source_target_pairs={{16,0},{32,16},{48,32},{64,48},{80,64},{96,80},{112,96},{128,112},... | collective-permute-start | bytes 393224 | tf_op jit(solution)/shard_map/ppermute | solution.py:17
  14.0 16.1 %collective-permute-start.1 = (f32[32,8,16]{2,1,0:T(8,128)S(1)}, f32[32,8,16]{2,1,0:T(8,128)S(1)}, u32[]{:S(2)}, u32[]{:S(2)}) collective-permute-start(f32[32,8,16]{2,1,0:T(8,128)S(1)} %get-tuple-element.74), channel_id=1, source_target_pairs={{0,1},{1,2},{2,3},{4,5},{5,6},{6,7},{8,9},{9,10},{10,11},{12,13},{... | collective-permute-start | bytes 49160 | tf_op jit(solution)/shard_map/ppermute | solution.py:25
  18.0 12.1 %collective-permute-start.2 = (f32[32,8,16]{2,1,0:T(8,128)S(1)}, f32[32,8,16]{2,1,0:T(8,128)S(1)}, u32[]{:S(2)}, u32[]{:S(2)}) collective-permute-start(f32[32,8,16]{2,1,0:T(8,128)S(1)} %get-tuple-element.75), channel_id=1, source_target_pairs={{1,0},{2,1},{3,2},{5,4},{6,5},{7,6},{9,8},{10,9},{11,10},{13,12},{... | collective-permute-start | bytes 49160 | tf_op jit(solution)/shard_map/ppermute | solution.py:28
  31.6 30.8 %copy-start = (s32[8]{0:T(128)S(1)}, s32[8]{0:T(128)}, u32[]{:S(2)}) copy-start(s32[8]{0:T(128)} %get-tuple-element.209) | copy-start | bytes 100 | tf_op jit(solution)/shard_map/while
  132.0 30.8 %copy-start = (s32[8]{0:T(128)S(1)}, s32[8]{0:T(128)}, u32[]{:S(2)}) copy-start(s32[8]{0:T(128)} %get-tuple-element.209) | copy-start | bytes 100 | tf_op jit(solution)/shard_map/while
Sparse Core Ops, SparseCore 0:
  238.1 73.0 reduce-scatter.4
where the time goes:
time: 319 us; the launch traced here: 318 us
  matrix products  135 us (42%)
  waiting for transfers between devices  78.3 us (25%)
  local copies, waits for them, and re-layouts  69.1 us (22%)
  between operations  13.5 us (4%)
  blocking collectives  10.5 us (3%)
  starting transfers between devices  6.54 us (2%)
  other arithmetic  3.84 us (1%)
    dot_general x2, matrix products, one_block(): jnp.einsum('spjt,skqt->spjkq', stacked, partners, precision=lax.Precision...  88 us
    unnamed x2, waiting for transfers between devices  73.2 us
    while x68, local copies, waits for them, and re-layouts  60 us
    dot_general x2, matrix products, one_block(): jnp.einsum('spjkq,pqd->skjd', product, pairing, precision=lax.Precision.H...  46.9 us
    all_gather x1, blocking collectives, shards(): lax.all_gather(velocity, 'az', axis=1, tiled=True)  10.5 us
  transfers between devices with their start and end apart: 4, of which 2 were waited for; matrix products, arithmetic and copies ran while one was open for 0% of the time, Pallas kernels for 0%

commit v1 on v0

v1 whole, which is shorter than its diff:
```python
import math

import jax
import jax.numpy as jnp
import numpy as np
from jax import lax
from jax.experimental import pallas as pl
from jax.experimental.pallas import tpu as pltpu
from jax.sharding import PartitionSpec as P

AZIM = 32
NBR = 8
MAXLAG = 16
LAGS = 33
MODES = 24
LEN = 128
ROWS = 72
MESH = pl.DeviceIdType.MESH
F32, BF16 = jnp.float32, jnp.bfloat16


def halves(table):
    high = table.astype(BF16)
    return high, (table - high.astype(np.float32)).astype(BF16)


def tables():
    mode, azim = np.arange(MODES), np.arange(AZIM)
    angle = 2 * np.pi * ((mode[:, None] * azim[None, :]) % AZIM) / AZIM
    parts = np.stack([np.cos(angle), np.sin(angle)])
    parts[1, 0], parts[1, 16] = 0, 0
    parts[:, 17:] = 0
    eye = np.eye(8)

    def over_stations(part):
        full = np.einsum("st,cmq->csmtq", eye, part)
        return full.reshape(2 * 8 * MODES, 8 * part.shape[2]).astype(np.float32)

    def left(table):
        high, low = halves(table)
        return np.concatenate([high, high, low], axis=1)

    def right(table):
        high, low = halves(table)
        return np.concatenate([high, high, low], axis=0)

    t = np.arange(LEN)
    omega = 2 * np.pi * ((t[:, None] * t[None, :]) % LEN) / LEN
    cos, sin = np.cos(omega), np.sin(omega)
    time = np.block([[cos, -sin], [-sin, -cos]]).astype(np.float32)
    lag = np.arange(-MAXLAG, MAXLAG + 1)
    omega = 2 * np.pi * ((lag[:, None] * t[None, :]) % LEN) / LEN
    cos, sin = np.cos(omega) / LEN, np.sin(omega) / LEN
    back = np.zeros((ROWS, 2 * LEN), np.float32)
    back[: 2 * LAGS] = np.block([[cos, -sin], [sin, cos]])
    slot = np.arange(16)
    angle = 2 * np.pi * ((slot[:, None] * azim[None, :]) % AZIM) / AZIM
    real, imag = 2 * np.cos(angle), -2 * np.sin(angle)
    real[0], imag[0] = 1, np.where(azim % 2 == 0, 1, -1)
    scale = 1.0 / (AZIM * math.sqrt(AZIM * 1024))
    last = np.concatenate([np.kron(eye, real), np.kron(eye, imag)], axis=1) * scale
    return (
        left(over_stations(parts)),
        left(over_stations(parts[:, :, :16])),
        right(time),
        left(back),
        right(last.astype(np.float32)),
    )


def split(value):
    high = value.astype(BF16)
    return high, (value - high.astype(F32)).astype(BF16)


def as_left(value):
    high, low = split(value)
    return jnp.concatenate([high, low, high], axis=1)


def as_right(value):
    high, low = split(value)
    return jnp.concatenate([high, low, high], axis=0)


def dot(left, right):
    return lax.dot_general(left, right, (((1,), (0,)), ((), ())), preferred_element_type=F32)


def lanes_of(shape):
    return lax.broadcasted_iota(jnp.int32, shape, len(shape) - 1)


def kernel(
    groups, vel, pres, offs, t_av, t_ap, t_w, t_wi, t_b, out,
    vbuf, pbuf, vraw, pack, hal, av, ap, w, wi, b, fv, fp, part, recv, rows_buf, turn_buf,
    local_sem, send_sem, vrecv, precv, zrecv, relay, hrecv, send2, recv2,
):
    gx, az, ta = lax.axis_index("gx"), lax.axis_index("az"), lax.axis_index("ta")
    y, c = az // 2, az % 2
    other = 1 - c
    partner = {"gx": gx, "az": 2 * y + other, "ta": ta}
    up = lax.rem(gx + groups - 1, groups)
    down = lax.rem(gx + 1, groups)
    mine = pl.ds(pl.multiple_of(az * 8, 8), 8)
    own_q = pl.ds(pl.multiple_of(c * 8, 8), 8)

    def device(a, t, g=gx):
        return (g, a, t)

    barrier = pltpu.get_barrier_semaphore()
    for step in range(1, 16):
        spot = lax.rem(az * 4 + ta + step, 16)
        pl.semaphore_signal(
            barrier, inc=1, device_id=device(spot // 4, spot % 4), device_id_type=MESH
        )

    for near in (up, down):
        pl.semaphore_signal(barrier, inc=1, device_id=device(az, ta, near), device_id_type=MESH)

    here = [
        pltpu.make_async_copy(vel, vraw, local_sem.at[0]),
        pltpu.make_async_copy(vel.at[pl.ds(8 * c, 8)], vbuf.at[:, mine], local_sem.at[1]),
        pltpu.make_async_copy(pres, pbuf.at[pl.ds(0, 16), own_q], local_sem.at[2]),
    ]
    for number, (source, target) in enumerate(
        [(t_av, av), (t_ap, ap), (t_w, w), (t_wi, wi), (t_b, b)]
    ):
        here.append(pltpu.make_async_copy(source, target, local_sem.at[3 + number]))
    for copy in here:
        copy.start()
    here[0].wait()

    lane8 = lanes_of((8, 128))
    for half in range(2):
        right = jnp.zeros((8, 128), F32)
        left = jnp.zeros((8, 128), F32)
        for j in range(8):
            here_lane = lane8 // 16 == j
            last = vraw[8 * half + j, :, 128:256]
            first = vraw[8 * half + j, :, 0:128]
            right = jnp.where(here_lane, pltpu.roll(last, (16 * j + 16) % 128, 1), right)
            left = jnp.where(here_lane, pltpu.roll(first, 16 * j, 1), left)
        pack[0, half] = right
        pack[1, half] = left

    pl.semaphore_wait(barrier, 17)

    def remote(source, target, send, receive, to):
        return pltpu.make_async_remote_copy(
            src_ref=source, dst_ref=target, send_sem=send, recv_sem=receive,
            device_id=to, device_id_type=MESH,
        )

    halo = [
        remote(
            pres.at[pl.ds(8 * n, 8)], pbuf.at[pl.ds(16 + 8 * n, 8), own_q],
            send_sem.at[n], zrecv.at[n], device(az, ta, up),
        )
        for n in range(2)
    ]

    @pl.when(gx > 0)
    def _():
        for copy in halo:
            copy.start()

    own_half = vel.at[pl.ds(8 * c, 8)]
    other_half = vel.at[pl.ds(8 * other, 8)]
    sends = [
        remote(own_half, vbuf.at[:, mine], send_sem.at[2], vrecv.at[0],
               device(2 * (1 - y) + c, ta)),
        remote(other_half, vbuf.at[:, mine], send_sem.at[3], vrecv.at[1],
               device(2 * (1 - y) + other, ta)),
        remote(other_half, vbuf.at[:, mine], send_sem.at[4], vrecv.at[2],
               device(2 * y + other, ta)),
        remote(pres, pbuf.at[pl.ds(0, 16), own_q], send_sem.at[5], precv.at[0],
               device(2 * y + other, ta)),
    ]
    for a in range(4):
        for side, shift in ((0, 1), (1, 3)):
            sends.append(
                remote(pack.at[side, a % 2], hal.at[side, mine],
                       send_sem.at[6 + 2 * a + side], hrecv.at[side, az],
                       device(a, lax.rem(ta + shift, 4)))
            )
    for copy in sends:
        copy.start()

    for copy in here[3:]:
        copy.wait()
    here[2].wait()
    sends[3].wait_recv()

    lane = lanes_of((384, 128))
    zero = jnp.zeros((384, 128), F32)

    def pressure(chunk):
        rows = pbuf[pl.ds(pl.multiple_of(8 * c + 8 * chunk, 8), 8)].reshape(128, 256)
        modes = dot(ap[...], as_right(rows))
        first, second = modes[:, :128], modes[:, 128:]
        windows = [
            jnp.where(lane < 96, first, zero),
            jnp.where(lane < 32, second, jnp.where(lane >= 96, first, zero)),
            jnp.where(lane >= 32, second, zero),
        ]
        for n, window in enumerate(windows):
            both = jnp.concatenate([window[:192], window[192:]], axis=1)
            spectrum = dot(as_left(both), w[...])
            fp[pl.ds(8 * chunk, 8), :, n * 256:(n + 1) * 256] = spectrum.reshape(8, MODES, 256)

    def velocity():
        lane = lanes_of((32, 128))
        low = jnp.where(ta > 0, hal[0], 0.0)
        high = jnp.where(ta < 3, hal[1], 0.0)
        columns = [[], [], []]
        for j in range(8):
            first, second = vbuf[j, :, 0:128], vbuf[j, :, 128:256]
            before = pltpu.roll(low, (112 - 16 * j) % 128, 1)
            after = pltpu.roll(high, (128 - 16 * j) % 128, 1)
            columns[0].append(jnp.where(lane < 112, first, before))
            columns[1].append(jnp.where(lane < 64, second, first))
            columns[2].append(jnp.where(lane >= 16, second, after))
        for n in range(3):
            rows = jnp.concatenate(columns[n], axis=0)
            modes = dot(av[...], as_right(rows))
            both = jnp.concatenate([modes[:192], modes[192:]], axis=1)
            spectrum = dot(as_left(both), w[...])
            fv[:, :, n * 256:(n + 1) * 256] = spectrum.reshape(8, MODES, 256)

    pressure(0)

    onward = [
        remote(
            pbuf.at[pl.ds(16 + 8 * n, 8), own_q], pbuf.at[pl.ds(16 + 8 * n, 8), own_q],
            send_sem.at[14 + n], relay.at[n], partner_id(gx, y, other, ta),
        )
        for n in range(2)
    ]

    here[1].wait()
    for copy in sends[:3]:
        copy.wait_recv()
    for side in range(2):
        for a in range(4):
            pltpu.make_async_copy(
                pack.at[0, 0], hal.at[side, pl.ds(8 * a, 8)], hrecv.at[side, a]
            ).wait()
    velocity()

    @pl.when(gx < groups - 1)
    def _():
        for n in range(2):
            halo[n].wait_recv()
            onward[n].start()
        for n in range(2):
            onward[n].wait_recv()

    @pl.when(gx == groups - 1)
    def _():
        pbuf[16:32] = jnp.zeros((16, 16, 256), F32)

    pressure(1)
    pressure(2)

    slot = 2 * ta + y

    def target_of(s):
        return device(2 * c + s // 4, s % 4)

    def outgoing(s):
        return remote(part.at[s], recv.at[slot], send2.at[s], recv2.at[slot], target_of(s))

    def deliver(s):
        to_self = jnp.logical_and(y == c, s == 4 * c + ta)

        @pl.when(to_self)
        def _():
            pltpu.make_async_copy(part.at[s], recv.at[slot], recv2.at[slot]).start()

        @pl.when(jnp.logical_not(to_self))
        def _():
            outgoing(s).start()

    def station(s, carry):
        v = [[fv[s, 8 * i:8 * i + 8, 128 * n:128 * n + 128] for n in range(6)] for i in range(3)]
        rows = []
        for k in range(NBR):
            near = s + offs[k]
            real, imag = [], []
            for i in range(3):
                re = im = None
                for n in range(3):
                    vr, vi = v[i][2 * n], v[i][2 * n + 1]
                    pr = fp[near, 8 * i:8 * i + 8, 256 * n:256 * n + 128]
                    pi = fp[near, 8 * i:8 * i + 8, 256 * n + 128:256 * n + 256]
                    one, two = vr * pr + vi * pi, vr * pi - vi * pr
                    re, im = (one, two) if n == 0 else (re + one, im + two)
                real.append(re)
                imag.append(im)
            re = jnp.concatenate([real[0] - imag[2], real[1]], axis=0)
            im = jnp.concatenate([imag[0] + real[2], imag[1]], axis=0)
            rows.append(jnp.concatenate([re, im], axis=1))
        grid = as_left(jnp.concatenate(rows, axis=0))
        part[s] = lax.dot_general(
            wi[...], grid, (((1,), (1,)), ((), ())), preferred_element_type=F32
        )

        @pl.when(s > 0)
        def _():
            deliver(s - 1)

        return carry

    lax.fori_loop(0, 8, station, 0)
    deliver(7)

    for n in range(8):
        pltpu.make_async_copy(part.at[0], recv.at[n], recv2.at[n]).wait()
    sums = []
    for upper in range(2):
        total = recv[upper]
        for n in range(1, 4):
            total = total + recv[2 * n + upper]
        sums.append(total)
    odd = lanes_of((ROWS, 128)) % 2 == 1
    total = sums[0] + jnp.where(odd, -sums[1], sums[1])
    rows_buf[0:ROWS] = dot(as_left(total), b[...])
    for k in range(NBR):
        for n in range(5):
            real = rows_buf[8 * n:8 * n + 8, 128 * (k // 4):128 * (k // 4) + 128]
            imag = rows_buf[LAGS + 8 * n:LAGS + 8 * n + 8, 256 + 128 * (k // 4):384 + 128 * (k // 4)]
            turn_buf[40 * k + 8 * n:40 * k + 8 * n + 8, :] = pltpu.roll(
                real + imag, (128 - 32 * (k % 4)) % 128, 1
            )
    for n in range(9):
        row = turn_buf[pl.ds(4 * n, 8, stride=40), :]
        for j in range(1, 4 if n < 8 else 1):
            turned = pltpu.roll(turn_buf[pl.ds(4 * n + j, 8, stride=40), :], 32 * j, 1)
            row = jnp.where(lane8 // 32 == j, turned, row)
        if n < 8:
            out[0, :, 128 * n:128 * n + 128] = row
        else:
            out[0, :, 1024:1056] = row[:, :32]

    for copy in sends:
        copy.wait_send()

    @pl.when(gx > 0)
    def _():
        for copy in halo:
            copy.wait_send()

    @pl.when(gx < groups - 1)
    def _():
        for copy in onward:
            copy.wait_send()

    def drain(s, carry):
        @pl.when(jnp.logical_not(jnp.logical_and(y == c, s == 4 * c + ta)))
        def _():
            outgoing(s).wait_send()

        return carry

    lax.fori_loop(0, 8, drain, 0)


def partner_id(gx, y, other, ta):
    return (gx, 2 * y + other, ta)


def solution(mesh):
    groups = mesh.shape["gx"]
    constants = tables()

    def shards(velocity, pressure, offsets):
        any_spec = pl.BlockSpec(memory_space=pltpu.HBM)
        dma = pltpu.SemaphoreType.DMA
        return pl.pallas_call(
            lambda *refs: kernel(groups, *refs),
            out_shape=jax.ShapeDtypeStruct((1, NBR, LAGS * AZIM), F32),
            in_specs=[any_spec, any_spec, pl.BlockSpec(memory_space=pltpu.SMEM)] + [any_spec] * 5,
            out_specs=pl.BlockSpec(memory_space=pltpu.VMEM),
            scratch_shapes=[
                pltpu.VMEM((8, AZIM, 256), F32),
                pltpu.VMEM((32, 16, 256), F32),
                pltpu.VMEM((16, 8, 256), F32),
                pltpu.VMEM((2, 2, 8, 128), F32),
                pltpu.VMEM((2, AZIM, 128), F32),
                *[pltpu.VMEM(table.shape, BF16) for table in constants],
                pltpu.VMEM((8, MODES, 768), F32),
                pltpu.VMEM((24, MODES, 768), F32),
                pltpu.VMEM((8, ROWS, 128), F32),
                pltpu.VMEM((8, ROWS, 128), F32),
                pltpu.VMEM((ROWS + 8, 512), F32),
                pltpu.VMEM((40 * NBR, 128), F32),
                dma((8,)), dma((16,)), dma((3,)), dma((1,)), dma((2,)), dma((2,)),
                dma((2, 4)), dma((8,)), dma((8,)),
            ],
            compiler_params=pltpu.CompilerParams(
                collective_id=0, has_side_effects=True, vmem_limit_bytes=67_000_000
            ),
            name="correlate",
        )(velocity, pressure, offsets, *[jnp.asarray(table) for table in constants])

    return jax.shard_map(
        shards,
        mesh=mesh,
        in_specs=(P("gx", "az", "ta"), P("gx", "az", "ta"), P()),
        out_specs=P(("gx", "az", "ta"), None, None),
        check_vma=False,
    )
```

time: 319 us -> 37 us (0.12)
  matrix products: 135 us -> 0 us
  waiting for transfers between devices: 78.3 us -> 0 us
  local copies, waits for them, and re-layouts: 69.1 us -> 1.39 us
  Pallas kernels: 0 us -> 34.9 us
  between operations: 13.5 us -> 0.01 us
  blocking collectives: 10.5 us -> 0 us
  starting transfers between devices: 6.54 us -> 0 us
  other arithmetic: 3.84 us -> 0 us
    dot_general x4 -> x0, matrix products: 135 us -> none  [the longest x2 88 us: one_block(): jnp.einsum('spjt,skqt->spjkq', stacked, partners, precision=lax.Precision...]
    unnamed x2 -> x0, waiting for transfers between devices: 73.2 us -> none
    while x68 -> x0, local copies, waits for them, and re-layouts: 60 us -> none
    pallas_call x0 -> x1, Pallas kernels: none -> 34.9 us  [shards(): pl.pallas_call(lambda *refs: kernel(groups, *refs), out_shape=jax.ShapeDt...]
    all_gather x1 -> x0, blocking collectives: 10.5 us -> none  [shards(): lax.all_gather(velocity, 'az', axis=1, tiled=True)]
    ppermute x3 -> x0, starting transfers between devices: 6.54 us -> none  [the longest x1 3.97 us: padded_2(): lax.ppermute(lax.slice_in_dim(block, block.shape[dim] - width, None, axis...]
    ppermute x3 -> x0, waiting for transfers between devices: 5.08 us -> none  [the longest x1 5.07 us: from_behind(): lax.ppermute(value, axis, [(source, source + steps) for source in range(l...]
    mul x2 -> x0, local copies, waits for them, and re-layouts: 3.66 us -> none  [shards(): partial_value = (totals * factor).reshape(sta_dev, NBR, LAGS * AZIM)]
  transfers between devices with their start and end apart: 4 -> 0, of which waited for: 2 -> 0; matrix products, arithmetic and copies ran while one was open for 0% -> 0% of each run, Pallas kernels for 0% -> 0%
where the time goes in v1:
time: 37 us; the launch traced here: 36.3 us
  Pallas kernels  34.9 us (94%)
  local copies, waits for them, and re-layouts  1.39 us (4%)
    pallas_call x1, Pallas kernels, shards(): pl.pallas_call(lambda *refs: kernel(groups, *refs), out_shape=jax.ShapeDt...  34.9 us
    unnamed x1, local copies, waits for them, and re-layouts  1.39 us

profile of v1, /device:TPU:1, one launch (start us, length us, event | category | flops | bytes accessed | tf_op | source)
XLA Modules:
  0.0 36.3 jit_solution(3840400152182551920)
XLA Ops:
  0.0 34.9 %correlate.1 = f32[1,8,1056]{2,1,0:T(8,128)} custom-call(f32[16,8,256]{2,1,0:T(8,128)} %refs_0_.1, f32[16,8,256]{2,1,0:T(8,128)} %refs_1_.1, s32[8]{0:T(128)} %refs_2_.1, bf16[384,768]{1,0:T(8,128)(2,1)} %constant.10.clone.refs_3_, bf16[384,384]{1,0:T(8,128)(2,1)} %constant.11.clone.refs_4_, bf16[768,256]{1,0:T(8,128)(2,1)} %constant.12.clone.refs_5_, ...), custom_call_target="tpu_custom_call" | custom-call | tf_op jit(solution)/shard_map/correlate/pallas_call | solution.py:380
  34.9 1.4 %copy.10 = f32[1,8,1056]{2,1,0:T(8,128)} copy(f32[1,8,1056]{2,1,0:T(8,128)} %correlate.1) | data formatting | bytes 67584

commit v2 on v1

--- a/solution.py
+++ b/solution.py
@@ -14,6 +14,7 @@
 LAGS = 33
 MODES = 24
 LEN = 128
+RING = 8
 ROWS = 72
 MESH = pl.DeviceIdType.MESH
 F32, BF16 = jnp.float32, jnp.bfloat16
@@ -92,16 +93,24 @@
 
 
 def kernel(
-    groups, vel, pres, offs, t_av, t_ap, t_w, t_wi, t_b, out,
-    vbuf, pbuf, vraw, pack, hal, av, ap, w, wi, b, fv, fp, part, recv, rows_buf, turn_buf,
-    local_sem, send_sem, vrecv, precv, zrecv, relay, hrecv, send2, recv2,
+    groups, vel, pres, t_offs, t_av, t_ap, t_w, t_wi, t_b, out,
+    offs, vbuf, pbuf, zbuf, vraw, pack, hal, av, ap, w, wi, b, fv, fp, part, recv, rows_buf, turn_buf,
+    local_sem, send_sem, vrecv, precv, zrecv, relay, hrecv, send2, recv2, ring_recv, ready, ring_ready, there,
 ):
     gx, az, ta = lax.axis_index("gx"), lax.axis_index("az"), lax.axis_index("ta")
     y, c = az // 2, az % 2
     other = 1 - c
     partner = {"gx": gx, "az": 2 * y + other, "ta": ta}
-    up = lax.rem(gx + groups - 1, groups)
-    down = lax.rem(gx + 1, groups)
+    opens = lax.rem(gx, RING) == 0
+    closes = lax.rem(gx, RING) == RING - 1
+    ahead_ring = gx < groups - RING
+    behind_ring = gx >= RING
+    up = jnp.where(opens, gx + RING - 1, gx - 1)
+    down = jnp.where(closes, gx - RING + 1, gx + 1)
+    has_up = jnp.logical_or(jnp.logical_not(opens), ahead_ring)
+    has_down = gx < groups - 1
+    lead = jnp.logical_and(gx == 0, az * 4 + ta == 0)
+    follows = jnp.logical_and(gx == 0, az * 4 + ta > 0)
     mine = pl.ds(pl.multiple_of(az * 8, 8), 8)
     own_q = pl.ds(pl.multiple_of(c * 8, 8), 8)
 
@@ -109,14 +118,24 @@
         return (g, a, t)
 
     barrier = pltpu.get_barrier_semaphore()
-    for step in range(1, 16):
-        spot = lax.rem(az * 4 + ta + step, 16)
+    across = [lax.rem(az + n, 4) for n in range(4)]
+    along = [lax.rem(ta + n, 4) for n in range(4)]
+    others = [(across[m], along[n]) for m in range(4) for n in (2, 1, 3, 0) if m + n > 0]
+
+    @pl.when(jnp.logical_not(lead))
+    def _():
+        for a, t in others:
+            pl.semaphore_signal(barrier, inc=1, device_id=device(a, t), device_id_type=MESH)
+
+    @pl.when(has_up)
+    def _():
+        pl.semaphore_signal(barrier, inc=1, device_id=device(az, ta, up), device_id_type=MESH)
+
+    @pl.when(jnp.logical_and(opens, behind_ring))
+    def _():
         pl.semaphore_signal(
-            barrier, inc=1, device_id=device(spot // 4, spot % 4), device_id_type=MESH
+            barrier, inc=1, device_id=device(az, ta, gx - RING), device_id_type=MESH
         )
-
-    for near in (up, down):
-        pl.semaphore_signal(barrier, inc=1, device_id=device(az, ta, near), device_id_type=MESH)
 
     here = [
         pltpu.make_async_copy(vel, vraw, local_sem.at[0]),
@@ -124,7 +143,7 @@
         pltpu.make_async_copy(pres, pbuf.at[pl.ds(0, 16), own_q], local_sem.at[2]),
     ]
     for number, (source, target) in enumerate(
-        [(t_av, av), (t_ap, ap), (t_w, w), (t_wi, wi), (t_b, b)]
+        [(t_av, av), (t_ap, ap), (t_w, w), (t_wi, wi), (t_b, b), (t_offs, offs)]
     ):
         here.append(pltpu.make_async_copy(source, target, local_sem.at[3 + number]))
     for copy in here:
@@ -144,7 +163,26 @@
         pack[0, half] = right
         pack[1, half] = left
 
-    pl.semaphore_wait(barrier, 17)
+    pl.semaphore_wait(
+        barrier,
+        15 + has_down.astype(jnp.int32) - follows.astype(jnp.int32)
+        + jnp.logical_and(opens, ahead_ring).astype(jnp.int32),
+    )
+
+    @pl.when(lead)
+    def _():
+        for a, t in others:
+            pl.semaphore_signal(there, inc=1, device_id=device(a, t), device_id_type=MESH)
+
+    @pl.when(has_down)
+    def _():
+        pl.semaphore_signal(ready, inc=1, device_id=device(az, ta, down), device_id_type=MESH)
+
+    @pl.when(jnp.logical_and(opens, ahead_ring))
+    def _():
+        pl.semaphore_signal(
+            ring_ready, inc=1, device_id=device(az, ta, gx + RING), device_id_type=MESH
+        )
 
     def remote(source, target, send, receive, to):
         return pltpu.make_async_remote_copy(
@@ -152,16 +190,25 @@
             device_id=to, device_id_type=MESH,
         )
 
-    halo = [
-        remote(
-            pres.at[pl.ds(8 * n, 8)], pbuf.at[pl.ds(16 + 8 * n, 8), own_q],
-            send_sem.at[n], zrecv.at[n], device(az, ta, up),
-        )
-        for n in range(2)
-    ]
-
-    @pl.when(gx > 0)
-    def _():
+    def halo_from(source):
+        return [
+            remote(
+                source.at[pl.ds(8 * n, 8)], pbuf.at[pl.ds(16 + 8 * n, 8), own_q],
+                send_sem.at[n], zrecv.at[n], device(az, ta, up),
+            )
+            for n in range(2)
+        ]
+
+    halo, halo_on = halo_from(pres), halo_from(zbuf)
+    to_ring = remote(
+        pres, zbuf, send_sem.at[16], ring_recv.at[0], device(az, ta, gx - RING)
+    )
+    hands_on = jnp.logical_and(opens, ahead_ring)
+    sends_ring = jnp.logical_and(opens, behind_ring)
+
+    @pl.when(jnp.logical_not(opens))
+    def _():
+        pl.semaphore_wait(ready, 1)
         for copy in halo:
             copy.start()
 
@@ -182,10 +229,23 @@
             sends.append(
                 remote(pack.at[side, a % 2], hal.at[side, mine],
                        send_sem.at[6 + 2 * a + side], hrecv.at[side, az],
-                       device(a, lax.rem(ta + shift, 4)))
+                       device(a, along[shift]))
             )
-    for copy in sends:
-        copy.start()
+    targets = [(2 * (1 - y) + c, ta), (2 * (1 - y) + other, ta)] + [(2 * y + other, ta)] * 2
+    targets += [(a, along[shift]) for a in range(4) for shift in (1, 3)]
+    to_lead = [jnp.logical_and(gx == 0, a * 4 + t == 0) for a, t in targets]
+    for copy, wait_for in zip(sends, to_lead):
+        @pl.when(jnp.logical_not(wait_for))
+        def _():
+            copy.start()
+
+    @pl.when(follows)
+    def _():
+        pl.semaphore_wait(there, 1)
+        for copy, waited_for in zip(sends, to_lead):
+            @pl.when(waited_for)
+            def _():
+                copy.start()
 
     for copy in here[3:]:
         copy.wait()
@@ -230,6 +290,11 @@
 
     pressure(0)
 
+    @pl.when(sends_ring)
+    def _():
+        pl.semaphore_wait(ring_ready, 1)
+        to_ring.start()
+
     onward = [
         remote(
             pbuf.at[pl.ds(16 + 8 * n, 8), own_q], pbuf.at[pl.ds(16 + 8 * n, 8), own_q],
@@ -248,20 +313,18 @@
             ).wait()
     velocity()
 
-    @pl.when(gx < groups - 1)
-    def _():
-        for n in range(2):
+    for n in range(2):
+        @pl.when(has_down)
+        def _():
             halo[n].wait_recv()
             onward[n].start()
-        for n in range(2):
             onward[n].wait_recv()
 
-    @pl.when(gx == groups - 1)
-    def _():
-        pbuf[16:32] = jnp.zeros((16, 16, 256), F32)
-
-    pressure(1)
-    pressure(2)
+        @pl.when(jnp.logical_not(has_down))
+        def _():
+            pbuf[16 + 8 * n:24 + 8 * n] = jnp.zeros((8, 16, 256), F32)
+
+        pressure(1 + n)
 
     slot = 2 * ta + y
 
@@ -311,6 +374,13 @@
             deliver(s - 1)
 
         return carry
+
+    @pl.when(hands_on)
+    def _():
+        pltpu.make_async_copy(pres, zbuf, ring_recv.at[0]).wait()
+        pl.semaphore_wait(ready, 1)
+        for copy in halo_on:
+            copy.start()
 
     lax.fori_loop(0, 8, station, 0)
     deliver(7)
@@ -346,12 +416,16 @@
     for copy in sends:
         copy.wait_send()
 
-    @pl.when(gx > 0)
-    def _():
-        for copy in halo:
+    @pl.when(has_up)
+    def _():
+        for copy in halo_on:
             copy.wait_send()
 
-    @pl.when(gx < groups - 1)
+    @pl.when(sends_ring)
+    def _():
+        to_ring.wait_send()
+
+    @pl.when(has_down)
     def _():
         for copy in onward:
             copy.wait_send()
@@ -380,11 +454,13 @@
         return pl.pallas_call(
             lambda *refs: kernel(groups, *refs),
             out_shape=jax.ShapeDtypeStruct((1, NBR, LAGS * AZIM), F32),
-            in_specs=[any_spec, any_spec, pl.BlockSpec(memory_space=pltpu.SMEM)] + [any_spec] * 5,
+            in_specs=[any_spec] * 8,
             out_specs=pl.BlockSpec(memory_space=pltpu.VMEM),
             scratch_shapes=[
+                pltpu.SMEM((NBR,), jnp.int32),
                 pltpu.VMEM((8, AZIM, 256), F32),
                 pltpu.VMEM((32, 16, 256), F32),
+                pltpu.VMEM((16, 8, 256), F32),
                 pltpu.VMEM((16, 8, 256), F32),
                 pltpu.VMEM((2, 2, 8, 128), F32),
                 pltpu.VMEM((2, AZIM, 128), F32),
@@ -395,8 +471,9 @@
                 pltpu.VMEM((8, ROWS, 128), F32),
                 pltpu.VMEM((ROWS + 8, 512), F32),
                 pltpu.VMEM((40 * NBR, 128), F32),
-                dma((8,)), dma((16,)), dma((3,)), dma((1,)), dma((2,)), dma((2,)),
+                dma((9,)), dma((17,)), dma((3,)), dma((1,)), dma((2,)), dma((2,)),
                 dma((2, 4)), dma((8,)), dma((8,)),
+                dma((1,)), *[pltpu.SemaphoreType.REGULAR] * 3,
             ],
             compiler_params=pltpu.CompilerParams(
                 collective_id=0, has_side_effects=True, vmem_limit_bytes=67_000_000

time: 37 us -> 28 us (0.76); the launches traced: 36.3 us -> 27.8 us
  Pallas kernels: 34.9 us -> 26.4 us
    pallas_call x1, Pallas kernels: 34.9 us -> 26.4 us  [shards(): pl.pallas_call(lambda *refs: kernel(groups, *refs), out_shape=jax.ShapeDt...]
where the time goes in v2:
time: 28 us; the launch traced here: 27.8 us
  Pallas kernels  26.4 us (94%)
  local copies, waits for them, and re-layouts  1.39 us (5%)
    pallas_call x1, Pallas kernels, shards(): pl.pallas_call(lambda *refs: kernel(groups, *refs), out_shape=jax.ShapeDt...  26.4 us
    unnamed x1, local copies, waits for them, and re-layouts  1.39 us

profile of v2, /device:TPU:1, one launch (start us, length us, event | category | flops | bytes accessed | tf_op | source)
XLA Modules:
  0.0 27.8 jit_solution(15479851040201856237)
XLA Ops:
  0.0 26.4 %correlate.1 = f32[1,8,1056]{2,1,0:T(8,128)} custom-call(f32[16,8,256]{2,1,0:T(8,128)} %refs_0_.1, f32[16,8,256]{2,1,0:T(8,128)} %refs_1_.1, s32[8]{0:T(128)} %refs_2_.1, bf16[384,768]{1,0:T(8,128)(2,1)} %constant.10.clone.refs_3_, bf16[384,384]{1,0:T(8,128)(2,1)} %constant.11.clone.refs_4_, bf16[768,256]{1,0:T(8,128)(2,1)} %constant.12.clone.refs_5_, ...), custom_call_target="tpu_custom_call" | custom-call | tf_op jit(solution)/shard_map/correlate/pallas_call | solution.py:454
  26.4 1.4 %copy.10 = f32[1,8,1056]{2,1,0:T(8,128)} copy(f32[1,8,1056]{2,1,0:T(8,128)} %correlate.1) | data formatting | bytes 67584

commit v3 on v2

--- a/solution.py
+++ b/solution.py
@@ -12,8 +12,8 @@
 NBR = 8
 MAXLAG = 16
 LAGS = 33
-MODES = 24
 LEN = 128
+HAND_TURN = 3
 RING = 8
 ROWS = 72
 MESH = pl.DeviceIdType.MESH
@@ -26,16 +26,19 @@
 
 
 def tables():
-    mode, azim = np.arange(MODES), np.arange(AZIM)
+    mode, azim = np.arange(17), np.arange(AZIM)
     angle = 2 * np.pi * ((mode[:, None] * azim[None, :]) % AZIM) / AZIM
     parts = np.stack([np.cos(angle), np.sin(angle)])
     parts[1, 0], parts[1, 16] = 0, 0
-    parts[:, 17:] = 0
     eye = np.eye(8)
 
-    def over_stations(part):
-        full = np.einsum("st,cmq->csmtq", eye, part)
-        return full.reshape(2 * 8 * MODES, 8 * part.shape[2]).astype(np.float32)
+    def over_stations(part, stations):
+        full = np.einsum("st,cmq->csmtq", np.eye(stations), part)
+        depth = stations * part.shape[2]
+        main = full[:, :, :16].reshape(2 * stations * 16, depth)
+        rest = np.zeros((16, depth))
+        rest[:stations] = full[0, :, 16].reshape(stations, depth)
+        return np.concatenate([main, rest]).astype(np.float32)
 
     def left(table):
         high, low = halves(table)
@@ -61,8 +64,8 @@
     scale = 1.0 / (AZIM * math.sqrt(AZIM * 1024))
     last = np.concatenate([np.kron(eye, real), np.kron(eye, imag)], axis=1) * scale
     return (
-        left(over_stations(parts)),
-        left(over_stations(parts[:, :, :16])),
+        left(over_stations(parts, 4)),
+        left(over_stations(parts[:, :, :16], 8)),
         right(time),
         left(back),
         right(last.astype(np.float32)),
@@ -94,7 +97,7 @@
 
 def kernel(
     groups, vel, pres, t_offs, t_av, t_ap, t_w, t_wi, t_b, out,
-    offs, vbuf, pbuf, zbuf, vraw, pack, hal, av, ap, w, wi, b, fv, fp, part, recv, rows_buf, turn_buf,
+    offs, vbuf, pbuf, zbuf, vraw, pack, hal, av, ap, w, wi, b, fv, fp, fv_16, fp_16, part, recv, rows_buf, turn_buf,
     local_sem, send_sem, vrecv, precv, zrecv, relay, hrecv, send2, recv2, ring_recv, ready, ring_ready, there,
 ):
     gx, az, ta = lax.axis_index("gx"), lax.axis_index("az"), lax.axis_index("ta")
@@ -111,6 +114,12 @@
     has_down = gx < groups - 1
     lead = jnp.logical_and(gx == 0, az * 4 + ta == 0)
     follows = jnp.logical_and(gx == 0, az * 4 + ta > 0)
+    last_block = gx == groups - 1
+    hands_on = jnp.logical_and(opens, ahead_ring)
+    sends_ring = jnp.logical_and(opens, behind_ring)
+    beside_lead = jnp.logical_and(gx == 0, jnp.logical_and(az == 1, ta == 0))
+    halo_to_lead = jnp.logical_and(gx == 1, az * 4 + ta == 0)
+    ring_to_lead = jnp.logical_and(gx == RING, az * 4 + ta == 0)
     mine = pl.ds(pl.multiple_of(az * 8, 8), 8)
     own_q = pl.ds(pl.multiple_of(c * 8, 8), 8)
 
@@ -127,15 +136,19 @@
         for a, t in others:
             pl.semaphore_signal(barrier, inc=1, device_id=device(a, t), device_id_type=MESH)
 
-    @pl.when(has_up)
-    def _():
-        pl.semaphore_signal(barrier, inc=1, device_id=device(az, ta, up), device_id_type=MESH)
-
-    @pl.when(jnp.logical_and(opens, behind_ring))
-    def _():
-        pl.semaphore_signal(
-            barrier, inc=1, device_id=device(az, ta, gx - RING), device_id_type=MESH
-        )
+    def tell(condition, semaphore, block):
+        @pl.when(condition)
+        def _():
+            pl.semaphore_signal(
+                semaphore, inc=1, device_id=device(az, ta, block), device_id_type=MESH
+            )
+
+    off_lead = jnp.logical_not(lead)
+    tell(jnp.logical_and(off_lead, jnp.logical_not(jnp.logical_or(closes, last_block))), barrier, gx + 1)
+    tell(jnp.logical_and(off_lead, hands_on), barrier, gx + RING)
+    tell(hands_on, barrier, up)
+    tell(halo_to_lead, barrier, 0)
+    tell(ring_to_lead, barrier, 0)
 
     here = [
         pltpu.make_async_copy(vel, vraw, local_sem.at[0]),
@@ -163,10 +176,17 @@
         pack[0, half] = right
         pack[1, half] = left
 
+    fv_16[...] = jnp.zeros_like(fv_16)
+    fp_16[...] = jnp.zeros_like(fp_16)
+
+    counted = [
+        jnp.logical_not(jnp.logical_or(opens, halo_to_lead)),
+        jnp.logical_and(closes, has_down),
+        jnp.logical_and(sends_ring, jnp.logical_not(ring_to_lead)),
+        lead, lead,
+    ]
     pl.semaphore_wait(
-        barrier,
-        15 + has_down.astype(jnp.int32) - follows.astype(jnp.int32)
-        + jnp.logical_and(opens, ahead_ring).astype(jnp.int32),
+        barrier, 15 - follows.astype(jnp.int32) + sum(one.astype(jnp.int32) for one in counted)
     )
 
     @pl.when(lead)
@@ -174,15 +194,9 @@
         for a, t in others:
             pl.semaphore_signal(there, inc=1, device_id=device(a, t), device_id_type=MESH)
 
-    @pl.when(has_down)
-    def _():
-        pl.semaphore_signal(ready, inc=1, device_id=device(az, ta, down), device_id_type=MESH)
-
-    @pl.when(jnp.logical_and(opens, ahead_ring))
-    def _():
-        pl.semaphore_signal(
-            ring_ready, inc=1, device_id=device(az, ta, gx + RING), device_id_type=MESH
-        )
+    tell(jnp.logical_and(closes, has_down), ready, down)
+    tell(lead, ready, 1)
+    tell(lead, ring_ready, RING)
 
     def remote(source, target, send, receive, to):
         return pltpu.make_async_remote_copy(
@@ -200,15 +214,16 @@
         ]
 
     halo, halo_on = halo_from(pres), halo_from(zbuf)
-    to_ring = remote(
-        pres, zbuf, send_sem.at[16], ring_recv.at[0], device(az, ta, gx - RING)
-    )
-    hands_on = jnp.logical_and(opens, ahead_ring)
-    sends_ring = jnp.logical_and(opens, behind_ring)
-
-    @pl.when(jnp.logical_not(opens))
-    def _():
-        pl.semaphore_wait(ready, 1)
+    to_ring = [
+        remote(
+            pres.at[pl.ds(8 * n, 8)], zbuf.at[pl.ds(8 * n, 8)],
+            send_sem.at[16 + n], ring_recv.at[n], device(az, ta, gx - RING),
+        )
+        for n in range(2)
+    ]
+
+    @pl.when(jnp.logical_not(jnp.logical_or(opens, halo_to_lead)))
+    def _():
         for copy in halo:
             copy.start()
 
@@ -239,61 +254,92 @@
         def _():
             copy.start()
 
-    @pl.when(follows)
-    def _():
+    @pl.when(jnp.logical_and(sends_ring, jnp.logical_not(ring_to_lead)))
+    def _():
+        for copy in to_ring:
+            copy.start()
+
+    def send_to_lead():
         pl.semaphore_wait(there, 1)
         for copy, waited_for in zip(sends, to_lead):
             @pl.when(waited_for)
             def _():
                 copy.start()
 
+    @pl.when(beside_lead)
+    def _():
+        send_to_lead()
+
     for copy in here[3:]:
         copy.wait()
     here[2].wait()
     sends[3].wait_recv()
 
-    lane = lanes_of((384, 128))
-    zero = jnp.zeros((384, 128), F32)
+    def spectra(windows, stations, target, target_16, start):
+        count = 16 * stations
+        parts = []
+        for window in windows:
+            cosines = jnp.concatenate([window[:count], window[2 * count:2 * count + 8]], axis=0)
+            sines = jnp.concatenate([window[count:2 * count], jnp.zeros((8, 128), F32)], axis=0)
+            parts.append(jnp.concatenate([cosines, sines], axis=1))
+        spectrum = dot(as_left(jnp.concatenate(parts, axis=0)), w[...])
+        for n in range(3):
+            rows = spectrum[n * (count + 8):(n + 1) * (count + 8)]
+            target[start:start + stations, :, n * 256:(n + 1) * 256] = (
+                rows[:count].reshape(stations, 16, 256)
+            )
+            for part_n in range(2):
+                first_row = target_16.shape[0] // 6 * (2 * n + part_n) + start
+                target_16[first_row:first_row + stations, 0, :] = (
+                    rows[count:count + stations, 128 * part_n:128 * part_n + 128]
+                )
 
     def pressure(chunk):
         rows = pbuf[pl.ds(pl.multiple_of(8 * c + 8 * chunk, 8), 8)].reshape(128, 256)
         modes = dot(ap[...], as_right(rows))
+        lane = lanes_of((272, 128))
         first, second = modes[:, :128], modes[:, 128:]
         windows = [
-            jnp.where(lane < 96, first, zero),
-            jnp.where(lane < 32, second, jnp.where(lane >= 96, first, zero)),
-            jnp.where(lane >= 32, second, zero),
+            jnp.where(lane < 96, first, 0.0),
+            jnp.where(lane < 32, second, jnp.where(lane >= 96, first, 0.0)),
+            jnp.where(lane >= 32, second, 0.0),
         ]
-        for n, window in enumerate(windows):
-            both = jnp.concatenate([window[:192], window[192:]], axis=1)
-            spectrum = dot(as_left(both), w[...])
-            fp[pl.ds(8 * chunk, 8), :, n * 256:(n + 1) * 256] = spectrum.reshape(8, MODES, 256)
+        spectra(windows, 8, fp, fp_16, 8 * chunk)
 
     def velocity():
         lane = lanes_of((32, 128))
         low = jnp.where(ta > 0, hal[0], 0.0)
         high = jnp.where(ta < 3, hal[1], 0.0)
-        columns = [[], [], []]
-        for j in range(8):
-            first, second = vbuf[j, :, 0:128], vbuf[j, :, 128:256]
-            before = pltpu.roll(low, (112 - 16 * j) % 128, 1)
-            after = pltpu.roll(high, (128 - 16 * j) % 128, 1)
-            columns[0].append(jnp.where(lane < 112, first, before))
-            columns[1].append(jnp.where(lane < 64, second, first))
-            columns[2].append(jnp.where(lane >= 16, second, after))
-        for n in range(3):
-            rows = jnp.concatenate(columns[n], axis=0)
+        for half in range(2):
+            columns = [[], [], []]
+            for j in range(4 * half, 4 * half + 4):
+                first, second = vbuf[j, :, 0:128], vbuf[j, :, 128:256]
+                before = pltpu.roll(low, (112 - 16 * j) % 128, 1)
+                after = pltpu.roll(high, (128 - 16 * j) % 128, 1)
+                columns[0].append(jnp.where(lane < 112, first, before))
+                columns[1].append(jnp.where(lane < 64, second, first))
+                columns[2].append(jnp.where(lane >= 16, second, after))
+            rows = jnp.concatenate([jnp.concatenate(col, axis=0) for col in columns], axis=1)
             modes = dot(av[...], as_right(rows))
-            both = jnp.concatenate([modes[:192], modes[192:]], axis=1)
-            spectrum = dot(as_left(both), w[...])
-            fv[:, :, n * 256:(n + 1) * 256] = spectrum.reshape(8, MODES, 256)
+            spectra([modes[:, 128 * n:128 * n + 128] for n in range(3)], 4, fv, fv_16, 4 * half)
 
     pressure(0)
 
-    @pl.when(sends_ring)
+    @pl.when(jnp.logical_and(follows, jnp.logical_not(beside_lead)))
+    def _():
+        send_to_lead()
+
+    @pl.when(halo_to_lead)
+    def _():
+        pl.semaphore_wait(ready, 1)
+        for copy in halo:
+            copy.start()
+
+    @pl.when(ring_to_lead)
     def _():
         pl.semaphore_wait(ring_ready, 1)
-        to_ring.start()
+        for copy in to_ring:
+            copy.start()
 
     onward = [
         remote(
@@ -302,6 +348,12 @@
         )
         for n in range(2)
     ]
+
+    for n in range(2):
+        @pl.when(has_down)
+        def _():
+            halo[n].wait_recv()
+            onward[n].start()
 
     here[1].wait()
     for copy in sends[:3]:
@@ -316,8 +368,6 @@
     for n in range(2):
         @pl.when(has_down)
         def _():
-            halo[n].wait_recv()
-            onward[n].start()
             onward[n].wait_recv()
 
         @pl.when(jnp.logical_not(has_down))
@@ -327,6 +377,12 @@
         pressure(1 + n)
 
     slot = 2 * ta + y
+
+    def station_at(turn):
+        ahead = jnp.where(turn < 2, 2, jnp.where(turn < 6, 1 + 2 * (turn % 2), 0))
+        core = jnp.where(turn < 2, turn, (turn // 2) % 2)
+        core = jnp.where(turn >= 6, turn % 2, core)
+        return 4 * core + lax.rem(ta + ahead, 4)
 
     def target_of(s):
         return device(2 * c + s // 4, s % 4)
@@ -345,8 +401,30 @@
         def _():
             outgoing(s).start()
 
-    def station(s, carry):
-        v = [[fv[s, 8 * i:8 * i + 8, 128 * n:128 * n + 128] for n in range(6)] for i in range(3)]
+    def hand_on(n):
+        if n == 0:
+            pl.semaphore_wait(ready, 1)
+        pltpu.make_async_copy(
+            pres.at[pl.ds(8 * n, 8)], zbuf.at[pl.ds(8 * n, 8)], ring_recv.at[n]
+        ).wait()
+        halo_on[n].start()
+
+    @pl.when(hands_on)
+    def _():
+        hand_on(0)
+
+    def station(turn, carry):
+        s = station_at(turn)
+
+        @pl.when(jnp.logical_and(hands_on, turn == HAND_TURN))
+        def _():
+            hand_on(1)
+
+        v = [
+            [fv[s, 0:8, 128 * n:128 * n + 128] for n in range(6)],
+            [fv[s, 8:16, 128 * n:128 * n + 128] for n in range(6)],
+            [fv_16[8 * n + s] for n in range(6)],
+        ]
         rows = []
         for k in range(NBR):
             near = s + offs[k]
@@ -355,8 +433,12 @@
                 re = im = None
                 for n in range(3):
                     vr, vi = v[i][2 * n], v[i][2 * n + 1]
-                    pr = fp[near, 8 * i:8 * i + 8, 256 * n:256 * n + 128]
-                    pi = fp[near, 8 * i:8 * i + 8, 256 * n + 128:256 * n + 256]
+                    if i < 2:
+                        pr = fp[near, 8 * i:8 * i + 8, 256 * n:256 * n + 128]
+                        pi = fp[near, 8 * i:8 * i + 8, 256 * n + 128:256 * n + 256]
+                    else:
+                        pr = fp_16[48 * n + near]
+                        pi = fp_16[48 * n + 24 + near]
                     one, two = vr * pr + vi * pi, vr * pi - vi * pr
                     re, im = (one, two) if n == 0 else (re + one, im + two)
                 real.append(re)
@@ -369,21 +451,14 @@
             wi[...], grid, (((1,), (1,)), ((), ())), preferred_element_type=F32
         )
 
-        @pl.when(s > 0)
-        def _():
-            deliver(s - 1)
+        @pl.when(turn > 0)
+        def _():
+            deliver(station_at(turn - 1))
 
         return carry
 
-    @pl.when(hands_on)
-    def _():
-        pltpu.make_async_copy(pres, zbuf, ring_recv.at[0]).wait()
-        pl.semaphore_wait(ready, 1)
-        for copy in halo_on:
-            copy.start()
-
     lax.fori_loop(0, 8, station, 0)
-    deliver(7)
+    deliver(station_at(7))
 
     for n in range(8):
         pltpu.make_async_copy(part.at[0], recv.at[n], recv2.at[n]).wait()
@@ -423,7 +498,8 @@
 
     @pl.when(sends_ring)
     def _():
-        to_ring.wait_send()
+        for copy in to_ring:
+            copy.wait_send()
 
     @pl.when(has_down)
     def _():
@@ -465,15 +541,17 @@
                 pltpu.VMEM((2, 2, 8, 128), F32),
                 pltpu.VMEM((2, AZIM, 128), F32),
                 *[pltpu.VMEM(table.shape, BF16) for table in constants],
-                pltpu.VMEM((8, MODES, 768), F32),
-                pltpu.VMEM((24, MODES, 768), F32),
+                pltpu.VMEM((8, 16, 768), F32),
+                pltpu.VMEM((24, 16, 768), F32),
+                pltpu.VMEM((48, 8, 128), F32),
+                pltpu.VMEM((144, 8, 128), F32),
                 pltpu.VMEM((8, ROWS, 128), F32),
                 pltpu.VMEM((8, ROWS, 128), F32),
                 pltpu.VMEM((ROWS + 8, 512), F32),
                 pltpu.VMEM((40 * NBR, 128), F32),
-                dma((9,)), dma((17,)), dma((3,)), dma((1,)), dma((2,)), dma((2,)),
+                dma((9,)), dma((18,)), dma((3,)), dma((1,)), dma((2,)), dma((2,)),
                 dma((2, 4)), dma((8,)), dma((8,)),
-                dma((1,)), *[pltpu.SemaphoreType.REGULAR] * 3,
+                dma((2,)), *[pltpu.SemaphoreType.REGULAR] * 3,
             ],
             compiler_params=pltpu.CompilerParams(
                 collective_id=0, has_side_effects=True, vmem_limit_bytes=67_000_000

time: 28 us -> 26.4 us (0.943)
  Pallas kernels: 26.4 us -> 24.8 us
    pallas_call x1, Pallas kernels: 26.4 us -> 24.8 us  [shards(): pl.pallas_call(lambda *refs: kernel(groups, *refs), out_shape=jax.ShapeDt...]
where the time goes in v3:
time: 26.4 us; the launch traced here: 26.2 us
  Pallas kernels  24.8 us (94%)
  local copies, waits for them, and re-layouts  1.39 us (5%)
    pallas_call x1, Pallas kernels, shards(): pl.pallas_call(lambda *refs: kernel(groups, *refs), out_shape=jax.ShapeDt...  24.8 us
    unnamed x1, local copies, waits for them, and re-layouts  1.39 us

profile of v3, /device:TPU:1, one launch (start us, length us, event | category | flops | bytes accessed | tf_op | source)
XLA Modules:
  0.0 26.2 jit_solution(3267164981532434489)
XLA Ops:
  0.0 24.8 %correlate.1 = f32[1,8,1056]{2,1,0:T(8,128)} custom-call(f32[16,8,256]{2,1,0:T(8,128)} %refs_0_.1, f32[16,8,256]{2,1,0:T(8,128)} %refs_1_.1, s32[8]{0:T(128)} %refs_2_.1, bf16[144,384]{1,0:T(8,128)(2,1)} %constant.10.clone.refs_3_, bf16[272,384]{1,0:T(8,128)(2,1)} %constant.11.clone.refs_4_, bf16[768,256]{1,0:T(8,128)(2,1)} %constant.12.clone.refs_5_, ...), custom_call_target="tpu_custom_call" | custom-call | tf_op jit(solution)/shard_map/correlate/pallas_call | solution.py:530
  24.8 1.4 %copy.10 = f32[1,8,1056]{2,1,0:T(8,128)} copy(f32[1,8,1056]{2,1,0:T(8,128)} %correlate.1) | data formatting | bytes 67584

commit v4 on v3

--- a/solution.py
+++ b/solution.py
@@ -13,7 +13,6 @@
 MAXLAG = 16
 LAGS = 33
 LEN = 128
-HAND_TURN = 3
 RING = 8
 ROWS = 72
 MESH = pl.DeviceIdType.MESH
@@ -98,7 +97,7 @@
 def kernel(
     groups, vel, pres, t_offs, t_av, t_ap, t_w, t_wi, t_b, out,
     offs, vbuf, pbuf, zbuf, vraw, pack, hal, av, ap, w, wi, b, fv, fp, fv_16, fp_16, part, recv, rows_buf, turn_buf,
-    local_sem, send_sem, vrecv, precv, zrecv, relay, hrecv, send2, recv2, ring_recv, ready, ring_ready, there,
+    local_sem, send_sem, vrecv, precv, zrecv, relay, hrecv, send2, recv2, ring_recv, ready, there,
 ):
     gx, az, ta = lax.axis_index("gx"), lax.axis_index("az"), lax.axis_index("ta")
     y, c = az // 2, az % 2
@@ -110,16 +109,14 @@
     behind_ring = gx >= RING
     up = jnp.where(opens, gx + RING - 1, gx - 1)
     down = jnp.where(closes, gx - RING + 1, gx + 1)
-    has_up = jnp.logical_or(jnp.logical_not(opens), ahead_ring)
     has_down = gx < groups - 1
     lead = jnp.logical_and(gx == 0, az * 4 + ta == 0)
     follows = jnp.logical_and(gx == 0, az * 4 + ta > 0)
     last_block = gx == groups - 1
-    hands_on = jnp.logical_and(opens, ahead_ring)
+    hands_on = jnp.logical_and(jnp.logical_and(opens, ahead_ring), y == 1)
     sends_ring = jnp.logical_and(opens, behind_ring)
     beside_lead = jnp.logical_and(gx == 0, jnp.logical_and(az == 1, ta == 0))
     halo_to_lead = jnp.logical_and(gx == 1, az * 4 + ta == 0)
-    ring_to_lead = jnp.logical_and(gx == RING, az * 4 + ta == 0)
     mine = pl.ds(pl.multiple_of(az * 8, 8), 8)
     own_q = pl.ds(pl.multiple_of(c * 8, 8), 8)
 
@@ -136,19 +133,23 @@
         for a, t in others:
             pl.semaphore_signal(barrier, inc=1, device_id=device(a, t), device_id_type=MESH)
 
-    def tell(condition, semaphore, block):
+    def tell(condition, semaphore, block, row=az):
         @pl.when(condition)
         def _():
             pl.semaphore_signal(
-                semaphore, inc=1, device_id=device(az, ta, block), device_id_type=MESH
+                semaphore, inc=1, device_id=device(row, ta, block), device_id_type=MESH
             )
 
     off_lead = jnp.logical_not(lead)
-    tell(jnp.logical_and(off_lead, jnp.logical_not(jnp.logical_or(closes, last_block))), barrier, gx + 1)
-    tell(jnp.logical_and(off_lead, hands_on), barrier, gx + RING)
-    tell(hands_on, barrier, up)
+    second = c == 1
+    told = jnp.logical_not(jnp.logical_or(closes, last_block))
+    tell(jnp.logical_and(off_lead, told), barrier, gx + 1)
+    tell(jnp.logical_and(second, told), barrier, gx + 1, 2 * y)
+    for upper in range(2):
+        tell(hands_on, barrier, gx + RING, 2 * upper + c)
+        tell(hands_on, barrier, up, 2 * upper + c)
+        tell(jnp.logical_and(hands_on, c == 0), barrier, up, 2 * upper + 1)
     tell(halo_to_lead, barrier, 0)
-    tell(ring_to_lead, barrier, 0)
 
     here = [
         pltpu.make_async_copy(vel, vraw, local_sem.at[0]),
@@ -181,9 +182,11 @@
 
     counted = [
         jnp.logical_not(jnp.logical_or(opens, halo_to_lead)),
+        jnp.logical_and(jnp.logical_not(opens), c == 0),
         jnp.logical_and(closes, has_down),
-        jnp.logical_and(sends_ring, jnp.logical_not(ring_to_lead)),
-        lead, lead,
+        jnp.logical_and(jnp.logical_and(closes, has_down), second),
+        sends_ring,
+        lead,
     ]
     pl.semaphore_wait(
         barrier, 15 - follows.astype(jnp.int32) + sum(one.astype(jnp.int32) for one in counted)
@@ -194,9 +197,9 @@
         for a, t in others:
             pl.semaphore_signal(there, inc=1, device_id=device(a, t), device_id_type=MESH)
 
-    tell(jnp.logical_and(closes, has_down), ready, down)
+    tell(jnp.logical_and(closes, has_down), ready, down, 2 + c)
+    tell(jnp.logical_and(jnp.logical_and(closes, has_down), second), ready, down, 2)
     tell(lead, ready, 1)
-    tell(lead, ring_ready, RING)
 
     def remote(source, target, send, receive, to):
         return pltpu.make_async_remote_copy(
@@ -204,28 +207,24 @@
             device_id=to, device_id_type=MESH,
         )
 
-    def halo_from(source):
+    def halo_from(source, row, sems):
         return [
             remote(
                 source.at[pl.ds(8 * n, 8)], pbuf.at[pl.ds(16 + 8 * n, 8), own_q],
-                send_sem.at[n], zrecv.at[n], device(az, ta, up),
+                send_sem.at[sems + n], zrecv.at[n * (1 + c)], device(row + n * (1 - c), ta, up),
             )
             for n in range(2)
         ]
 
-    halo, halo_on = halo_from(pres), halo_from(zbuf)
+    halo = halo_from(pres, az, 0)
+    halo_on = [halo_from(zbuf.at[upper], 2 * upper + c, 18 * (1 - upper)) for upper in range(2)]
     to_ring = [
         remote(
-            pres.at[pl.ds(8 * n, 8)], zbuf.at[pl.ds(8 * n, 8)],
-            send_sem.at[16 + n], ring_recv.at[n], device(az, ta, gx - RING),
+            pres.at[pl.ds(8 * n, 8)], zbuf.at[y, pl.ds(8 * n, 8)],
+            send_sem.at[16 + n], ring_recv.at[y, n], device(2 + c, ta, gx - RING),
         )
         for n in range(2)
     ]
-
-    @pl.when(jnp.logical_not(jnp.logical_or(opens, halo_to_lead)))
-    def _():
-        for copy in halo:
-            copy.start()
 
     own_half = vel.at[pl.ds(8 * c, 8)]
     other_half = vel.at[pl.ds(8 * other, 8)]
@@ -249,12 +248,23 @@
     targets = [(2 * (1 - y) + c, ta), (2 * (1 - y) + other, ta)] + [(2 * y + other, ta)] * 2
     targets += [(a, along[shift]) for a in range(4) for shift in (1, 3)]
     to_lead = [jnp.logical_and(gx == 0, a * 4 + t == 0) for a, t in targets]
-    for copy, wait_for in zip(sends, to_lead):
-        @pl.when(jnp.logical_not(wait_for))
-        def _():
+    def start(numbers):
+        for n in numbers:
+            @pl.when(jnp.logical_not(to_lead[n]))
+            def _():
+                sends[n].start()
+
+    start(range(4, 12))
+    start((0, 1))
+
+    @pl.when(jnp.logical_not(jnp.logical_or(opens, halo_to_lead)))
+    def _():
+        for copy in halo:
             copy.start()
 
-    @pl.when(jnp.logical_and(sends_ring, jnp.logical_not(ring_to_lead)))
+    start((3, 2))
+
+    @pl.when(sends_ring)
     def _():
         for copy in to_ring:
             copy.start()
@@ -335,26 +345,30 @@
         for copy in halo:
             copy.start()
 
-    @pl.when(ring_to_lead)
-    def _():
-        pl.semaphore_wait(ring_ready, 1)
-        for copy in to_ring:
-            copy.start()
-
-    onward = [
-        remote(
-            pbuf.at[pl.ds(16 + 8 * n, 8), own_q], pbuf.at[pl.ds(16 + 8 * n, 8), own_q],
-            send_sem.at[14 + n], relay.at[n], partner_id(gx, y, other, ta),
-        )
-        for n in range(2)
-    ]
-
-    for n in range(2):
-        @pl.when(has_down)
-        def _():
-            halo[n].wait_recv()
-            onward[n].start()
-
+    onward = remote(
+        pbuf.at[pl.ds(16, 8), own_q], pbuf.at[pl.ds(16, 8), own_q],
+        send_sem.at[14], relay.at[0], partner_id(gx, y, other, ta),
+    )
+
+    def arrived(n):
+        pltpu.make_async_copy(
+            pres.at[pl.ds(0, 8)], pbuf.at[pl.ds(16, 8), own_q], zrecv.at[n]
+        ).wait()
+
+    @pl.when(has_down)
+    def _():
+        arrived(0)
+        onward.start()
+
+    @pl.when(jnp.logical_not(has_down))
+    def _():
+        pbuf[16:32] = jnp.zeros((16, 16, 256), F32)
+
+    @pl.when(jnp.logical_and(has_down, second))
+    def _():
+        onward.wait_recv()
+
+    pressure(1)
     here[1].wait()
     for copy in sends[:3]:
         copy.wait_recv()
@@ -365,16 +379,16 @@
             ).wait()
     velocity()
 
-    for n in range(2):
-        @pl.when(has_down)
-        def _():
-            onward[n].wait_recv()
-
-        @pl.when(jnp.logical_not(has_down))
-        def _():
-            pbuf[16 + 8 * n:24 + 8 * n] = jnp.zeros((8, 16, 256), F32)
-
-        pressure(1 + n)
+    @pl.when(jnp.logical_and(has_down, c == 0))
+    def _():
+        onward.wait_recv()
+
+    @pl.when(jnp.logical_and(has_down, second))
+    def _():
+        arrived(1)
+        arrived(2)
+
+    pressure(2)
 
     slot = 2 * ta + y
 
@@ -403,22 +417,20 @@
 
     def hand_on(n):
         if n == 0:
-            pl.semaphore_wait(ready, 1)
-        pltpu.make_async_copy(
-            pres.at[pl.ds(8 * n, 8)], zbuf.at[pl.ds(8 * n, 8)], ring_recv.at[n]
-        ).wait()
-        halo_on[n].start()
-
-    @pl.when(hands_on)
-    def _():
-        hand_on(0)
+            pl.semaphore_wait(ready, 4 - 2 * c)
+        for upper in (1, 0):
+            pltpu.make_async_copy(
+                pres.at[pl.ds(8 * n, 8)], zbuf.at[upper, pl.ds(8 * n, 8)], ring_recv.at[upper, n]
+            ).wait()
+            halo_on[upper][n].start()
 
     def station(turn, carry):
         s = station_at(turn)
 
-        @pl.when(jnp.logical_and(hands_on, turn == HAND_TURN))
-        def _():
-            hand_on(1)
+        for n in range(2):
+            @pl.when(jnp.logical_and(hands_on, turn == 3 * n + 2 * (gx == 0).astype(jnp.int32)))
+            def _():
+                hand_on(n)
 
         v = [
             [fv[s, 0:8, 128 * n:128 * n + 128] for n in range(6)],
@@ -491,9 +503,14 @@
     for copy in sends:
         copy.wait_send()
 
-    @pl.when(has_up)
-    def _():
-        for copy in halo_on:
+    @pl.when(jnp.logical_not(opens))
+    def _():
+        for copy in halo:
+            copy.wait_send()
+
+    @pl.when(hands_on)
+    def _():
+        for copy in halo_on[0] + halo_on[1]:
             copy.wait_send()
 
     @pl.when(sends_ring)
@@ -503,8 +520,7 @@
 
     @pl.when(has_down)
     def _():
-        for copy in onward:
-            copy.wait_send()
+        onward.wait_send()
 
     def drain(s, carry):
         @pl.when(jnp.logical_not(jnp.logical_and(y == c, s == 4 * c + ta)))
@@ -536,7 +552,7 @@
                 pltpu.SMEM((NBR,), jnp.int32),
                 pltpu.VMEM((8, AZIM, 256), F32),
                 pltpu.VMEM((32, 16, 256), F32),
-                pltpu.VMEM((16, 8, 256), F32),
+                pltpu.VMEM((2, 16, 8, 256), F32),
                 pltpu.VMEM((16, 8, 256), F32),
                 pltpu.VMEM((2, 2, 8, 128), F32),
                 pltpu.VMEM((2, AZIM, 128), F32),
@@ -549,9 +565,9 @@
                 pltpu.VMEM((8, ROWS, 128), F32),
                 pltpu.VMEM((ROWS + 8, 512), F32),
                 pltpu.VMEM((40 * NBR, 128), F32),
-                dma((9,)), dma((18,)), dma((3,)), dma((1,)), dma((2,)), dma((2,)),
+                dma((9,)), dma((20,)), dma((3,)), dma((1,)), dma((3,)), dma((1,)),
                 dma((2, 4)), dma((8,)), dma((8,)),
-                dma((2,)), *[pltpu.SemaphoreType.REGULAR] * 3,
+                dma((2, 2)), *[pltpu.SemaphoreType.REGULAR] * 2,
             ],
             compiler_params=pltpu.CompilerParams(
                 collective_id=0, has_side_effects=True, vmem_limit_bytes=67_000_000

time: 26.4 us -> 25.8 us (0.977)
  Pallas kernels: 24.8 us -> 24.2 us
    pallas_call x1, Pallas kernels: 24.8 us -> 24.2 us  [shards(): pl.pallas_call(lambda *refs: kernel(groups, *refs), out_shape=jax.ShapeDt...]
where the time goes in v4:
time: 25.8 us; the launch traced here: 25.6 us
  Pallas kernels  24.2 us (94%)
  local copies, waits for them, and re-layouts  1.39 us (5%)
    pallas_call x1, Pallas kernels, shards(): pl.pallas_call(lambda *refs: kernel(groups, *refs), out_shape=jax.ShapeDt...  24.2 us
    unnamed x1, local copies, waits for them, and re-layouts  1.39 us

profile of v4, /device:TPU:1, one launch (start us, length us, event | category | flops | bytes accessed | tf_op | source)
XLA Modules:
  0.0 25.6 jit_solution(15873848448315105803)
XLA Ops:
  0.0 24.2 %correlate.1 = f32[1,8,1056]{2,1,0:T(8,128)} custom-call(f32[16,8,256]{2,1,0:T(8,128)} %refs_0_.1, f32[16,8,256]{2,1,0:T(8,128)} %refs_1_.1, s32[8]{0:T(128)} %refs_2_.1, bf16[144,384]{1,0:T(8,128)(2,1)} %constant.10.clone.refs_3_, bf16[272,384]{1,0:T(8,128)(2,1)} %constant.11.clone.refs_4_, bf16[768,256]{1,0:T(8,128)(2,1)} %constant.12.clone.refs_5_, ...), custom_call_target="tpu_custom_call" | custom-call | tf_op jit(solution)/shard_map/correlate/pallas_call | solution.py:546
  24.2 1.4 %copy.10 = f32[1,8,1056]{2,1,0:T(8,128)} copy(f32[1,8,1056]{2,1,0:T(8,128)} %correlate.1) | data formatting | bytes 67584

commit v5 on v4

--- a/solution.py
+++ b/solution.py
@@ -14,6 +14,7 @@
 LAGS = 33
 LEN = 128
 RING = 8
+HAND_PAIRS = ((2, 0), (4, 4))
 ROWS = 72
 MESH = pl.DeviceIdType.MESH
 F32, BF16 = jnp.float32, jnp.bfloat16
@@ -424,14 +425,8 @@
             ).wait()
             halo_on[upper][n].start()
 
-    def station(turn, carry):
+    def station(turn):
         s = station_at(turn)
-
-        for n in range(2):
-            @pl.when(jnp.logical_and(hands_on, turn == 3 * n + 2 * (gx == 0).astype(jnp.int32)))
-            def _():
-                hand_on(n)
-
         v = [
             [fv[s, 0:8, 128 * n:128 * n + 128] for n in range(6)],
             [fv[s, 8:16, 128 * n:128 * n + 128] for n in range(6)],
@@ -463,14 +458,27 @@
             wi[...], grid, (((1,), (1,)), ((), ())), preferred_element_type=F32
         )
 
-        @pl.when(turn > 0)
+    def hand_on_at(pair):
+        for n, (at_first, elsewhere) in enumerate(HAND_PAIRS):
+            @pl.when(jnp.logical_and(hands_on, pair == jnp.where(gx == 0, at_first, elsewhere)))
+            def _():
+                hand_on(n)
+
+    def stations(pair, carry):
+        hand_on_at(pair)
+        station(2 * pair)
+        station(2 * pair + 1)
+
+        @pl.when(pair > 0)
         def _():
-            deliver(station_at(turn - 1))
-
+            deliver(station_at(2 * pair - 1))
+
+        deliver(station_at(2 * pair))
         return carry
 
-    lax.fori_loop(0, 8, station, 0)
+    lax.fori_loop(0, 4, stations, 0)
     deliver(station_at(7))
+    hand_on_at(4)
 
     for n in range(8):
         pltpu.make_async_copy(part.at[0], recv.at[n], recv2.at[n]).wait()
@@ -570,10 +578,10 @@
                 dma((2, 2)), *[pltpu.SemaphoreType.REGULAR] * 2,
             ],
             compiler_params=pltpu.CompilerParams(
-                collective_id=0, has_side_effects=True, vmem_limit_bytes=67_000_000
+                collective_id=0, has_side_effects=True, vmem_limit_bytes=48 << 20
             ),
             name="correlate",
-        )(velocity, pressure, offsets, *[jnp.asarray(table) for table in constants])
+        )(*[pltpu.with_memory_space_constraint(x, pltpu.HBM) for x in (velocity, pressure, offsets, *[jnp.asarray(table) for table in constants])])
 
     return jax.shard_map(
         shards,

time: 25.8 us -> 23.7 us (0.919)
  Pallas kernels: 24.2 us -> 22.9 us
  local copies, waits for them, and re-layouts: 1.39 us -> 0.62 us
    pallas_call x1, Pallas kernels: 24.2 us -> 22.9 us  [shards(): pl.pallas_call(lambda *refs: kernel(groups, *refs), out_shape=jax.ShapeDt...]
    unnamed x1, local copies, waits for them, and re-layouts: 1.39 us -> 0.62 us
where the time goes in v5:
time: 23.7 us; the launch traced here: 23.6 us
  Pallas kernels  22.9 us (97%)
  local copies, waits for them, and re-layouts  0.62 us (3%)
    pallas_call x1, Pallas kernels, shards(): pl.pallas_call(lambda *refs: kernel(groups, *refs), out_shape=jax.ShapeDt...  22.9 us
    unnamed x1, local copies, waits for them, and re-layouts  0.62 us

profile of v5, /device:TPU:1, one launch (start us, length us, event | category | flops | bytes accessed | tf_op | source)
XLA Modules:
  0.0 23.6 jit_solution(4017115199929268216)
XLA Ops:
  0.0 22.9 %correlate.1 = f32[1,8,1056]{2,1,0:T(8,128)S(1)} custom-call(f32[16,8,256]{2,1,0:T(8,128)} %refs_0_.1, f32[16,8,256]{2,1,0:T(8,128)} %refs_1_.1, s32[8]{0:T(128)} %refs_2_.1, bf16[144,384]{1,0:T(8,128)(2,1)} %constant.10.clone.refs_3_, bf16[272,384]{1,0:T(8,128)(2,1)} %constant.11.clone.refs_4_, bf16[768,256]{1,0:T(8,128)(2,1)} %constant.12.clone.refs_5_, ...), custom_call_target="tpu_custom_call" | custom-call | tf_op jit(solution)/shard_map/correlate/pallas_call | solution.py:554
  23.0 0.6 %copy.10 = f32[1,8,1056]{2,1,0:T(8,128)} copy(f32[1,8,1056]{2,1,0:T(8,128)S(1)} %correlate.1) | data formatting | bytes 67584

commit v6 on v5

--- a/solution.py
+++ b/solution.py
@@ -163,6 +163,43 @@
         here.append(pltpu.make_async_copy(source, target, local_sem.at[3 + number]))
     for copy in here:
         copy.start()
+    def remote(source, target, send, receive, to):
+        return pltpu.make_async_remote_copy(
+            src_ref=source, dst_ref=target, send_sem=send, recv_sem=receive,
+            device_id=to, device_id_type=MESH,
+        )
+
+    counted = [
+        jnp.logical_not(jnp.logical_or(opens, halo_to_lead)),
+        jnp.logical_and(jnp.logical_not(opens), c == 0),
+        jnp.logical_and(closes, has_down),
+        jnp.logical_and(jnp.logical_and(closes, has_down), second),
+        sends_ring,
+        lead,
+    ]
+    count = 15 - follows.astype(jnp.int32) + sum(one.astype(jnp.int32) for one in counted)
+    own_half = vel.at[pl.ds(8 * c, 8)]
+    other_half = vel.at[pl.ds(8 * other, 8)]
+    sends = [
+        remote(own_half, vbuf.at[:, mine], send_sem.at[2], vrecv.at[0],
+               device(2 * (1 - y) + c, ta)),
+        remote(other_half, vbuf.at[:, mine], send_sem.at[3], vrecv.at[1],
+               device(2 * (1 - y) + other, ta)),
+        remote(other_half, vbuf.at[:, mine], send_sem.at[4], vrecv.at[2],
+               device(2 * y + other, ta)),
+        remote(pres, pbuf.at[pl.ds(0, 16), own_q], send_sem.at[5], precv.at[0],
+               device(2 * y + other, ta)),
+    ]
+
+    @pl.when(lead)
+    def _():
+        pl.semaphore_wait(barrier, count)
+        for a, t in others:
+            pl.semaphore_signal(there, inc=1, device_id=device(a, t), device_id_type=MESH)
+        pl.semaphore_signal(ready, inc=1, device_id=device(az, ta, 1), device_id_type=MESH)
+        for n in (0, 1, 3, 2):
+            sends[n].start()
+
     here[0].wait()
 
     lane8 = lanes_of((8, 128))
@@ -181,32 +218,12 @@
     fv_16[...] = jnp.zeros_like(fv_16)
     fp_16[...] = jnp.zeros_like(fp_16)
 
-    counted = [
-        jnp.logical_not(jnp.logical_or(opens, halo_to_lead)),
-        jnp.logical_and(jnp.logical_not(opens), c == 0),
-        jnp.logical_and(closes, has_down),
-        jnp.logical_and(jnp.logical_and(closes, has_down), second),
-        sends_ring,
-        lead,
-    ]
-    pl.semaphore_wait(
-        barrier, 15 - follows.astype(jnp.int32) + sum(one.astype(jnp.int32) for one in counted)
-    )
-
-    @pl.when(lead)
-    def _():
-        for a, t in others:
-            pl.semaphore_signal(there, inc=1, device_id=device(a, t), device_id_type=MESH)
+    @pl.when(off_lead)
+    def _():
+        pl.semaphore_wait(barrier, count)
 
     tell(jnp.logical_and(closes, has_down), ready, down, 2 + c)
     tell(jnp.logical_and(jnp.logical_and(closes, has_down), second), ready, down, 2)
-    tell(lead, ready, 1)
-
-    def remote(source, target, send, receive, to):
-        return pltpu.make_async_remote_copy(
-            src_ref=source, dst_ref=target, send_sem=send, recv_sem=receive,
-            device_id=to, device_id_type=MESH,
-        )
 
     def halo_from(source, row, sems):
         return [
@@ -227,18 +244,6 @@
         for n in range(2)
     ]
 
-    own_half = vel.at[pl.ds(8 * c, 8)]
-    other_half = vel.at[pl.ds(8 * other, 8)]
-    sends = [
-        remote(own_half, vbuf.at[:, mine], send_sem.at[2], vrecv.at[0],
-               device(2 * (1 - y) + c, ta)),
-        remote(other_half, vbuf.at[:, mine], send_sem.at[3], vrecv.at[1],
-               device(2 * (1 - y) + other, ta)),
-        remote(other_half, vbuf.at[:, mine], send_sem.at[4], vrecv.at[2],
-               device(2 * y + other, ta)),
-        remote(pres, pbuf.at[pl.ds(0, 16), own_q], send_sem.at[5], precv.at[0],
-               device(2 * y + other, ta)),
-    ]
     for a in range(4):
         for side, shift in ((0, 1), (1, 3)):
             sends.append(
@@ -251,11 +256,17 @@
     to_lead = [jnp.logical_and(gx == 0, a * 4 + t == 0) for a, t in targets]
     def start(numbers):
         for n in numbers:
-            @pl.when(jnp.logical_not(to_lead[n]))
+            begun = lead if n < 4 else False
+
+            @pl.when(jnp.logical_not(jnp.logical_or(to_lead[n], begun)))
             def _():
                 sends[n].start()
 
     start(range(4, 12))
+    @pl.when(sends_ring)
+    def _():
+        to_ring[0].start()
+
     start((0, 1))
 
     @pl.when(jnp.logical_not(jnp.logical_or(opens, halo_to_lead)))
@@ -267,8 +278,7 @@
 
     @pl.when(sends_ring)
     def _():
-        for copy in to_ring:
-            copy.start()
+        to_ring[1].start()
 
     def send_to_lead():
         pl.semaphore_wait(there, 1)

time: 23.7 us -> 23.4 us (0.987)
    pallas_call x1, Pallas kernels: 22.9 us -> 22.7 us  [shards(): pl.pallas_call(lambda *refs: kernel(groups, *refs), out_shape=jax.ShapeDt...]
where the time goes in v6:
time: 23.4 us; the launch traced here: 23.3 us
  Pallas kernels  22.7 us (97%)
  local copies, waits for them, and re-layouts  0.62 us (3%)
    pallas_call x1, Pallas kernels, shards(): pl.pallas_call(lambda *refs: kernel(groups, *refs), out_shape=jax.ShapeDt...  22.7 us
    unnamed x1, local copies, waits for them, and re-layouts  0.62 us

profile of v6, /device:TPU:1, one launch (start us, length us, event | category | flops | bytes accessed | tf_op | source)
XLA Modules:
  0.0 23.3 jit_solution(12718900122698185704)
XLA Ops:
  0.0 22.7 %correlate.1 = f32[1,8,1056]{2,1,0:T(8,128)S(1)} custom-call(f32[16,8,256]{2,1,0:T(8,128)} %refs_0_.1, f32[16,8,256]{2,1,0:T(8,128)} %refs_1_.1, s32[8]{0:T(128)} %refs_2_.1, bf16[144,384]{1,0:T(8,128)(2,1)} %constant.10.clone.refs_3_, bf16[272,384]{1,0:T(8,128)(2,1)} %constant.11.clone.refs_4_, bf16[768,256]{1,0:T(8,128)(2,1)} %constant.12.clone.refs_5_, ...), custom_call_target="tpu_custom_call" | custom-call | tf_op jit(solution)/shard_map/correlate/pallas_call | solution.py:564
  22.7 0.6 %copy.10 = f32[1,8,1056]{2,1,0:T(8,128)} copy(f32[1,8,1056]{2,1,0:T(8,128)S(1)} %correlate.1) | data formatting | bytes 67584

commit v7 on v6

--- a/solution.py
+++ b/solution.py
@@ -15,7 +15,7 @@
 LEN = 128
 RING = 8
 HAND_PAIRS = ((2, 0), (4, 4))
-ROWS = 72
+ROWS = 66
 MESH = pl.DeviceIdType.MESH
 F32, BF16 = jnp.float32, jnp.bfloat16
 

time: 23.4 us -> 23.2 us (level)
  Pallas kernels: 22.7 us -> 22.4 us
where the time goes in v7:
time: 23.2 us; the launch traced here: 23.1 us
  Pallas kernels  22.4 us (97%)
  local copies, waits for them, and re-layouts  0.62 us (3%)
    pallas_call x1, Pallas kernels, shards(): pl.pallas_call(lambda *refs: kernel(groups, *refs), out_shape=jax.ShapeDt...  22.4 us
    unnamed x1, local copies, waits for them, and re-layouts  0.62 us

profile of v7, /device:TPU:1, one launch (start us, length us, event | category | flops | bytes accessed | tf_op | source)
XLA Modules:
  0.0 23.1 jit_solution(9035565868817917905)
XLA Ops:
  0.0 22.4 %correlate.1 = f32[1,8,1056]{2,1,0:T(8,128)S(1)} custom-call(f32[16,8,256]{2,1,0:T(8,128)} %refs_0_.1, f32[16,8,256]{2,1,0:T(8,128)} %refs_1_.1, s32[8]{0:T(128)} %refs_2_.1, bf16[144,384]{1,0:T(8,128)(2,1)} %constant.10.clone.refs_3_, bf16[272,384]{1,0:T(8,128)(2,1)} %constant.11.clone.refs_4_, bf16[768,256]{1,0:T(8,128)(2,1)} %constant.12.clone.refs_5_, ...), custom_call_target="tpu_custom_call" | custom-call | tf_op jit(solution)/shard_map/correlate/pallas_call | solution.py:564
  22.4 0.6 %copy.10 = f32[1,8,1056]{2,1,0:T(8,128)} copy(f32[1,8,1056]{2,1,0:T(8,128)S(1)} %correlate.1) | data formatting | bytes 67584
